TPU v7x, 32 devices: a whole 2x2x4 slice. The times are simulated.
32 devices in a mesh: paths: 4 (over y, core), factors: 8 (over z, x).
Axes of the slice: x: 2, y: 2, z: 4, core: 2. Of those that a mesh axis runs over, the one named last changes fastest.
Arguments:
- x_start: float32 [512, 2048], P('factors', 'paths'), may hold values from -3 to 3
- shocks: float32 [4, 512, 2048], P(None, 'factors', 'paths'), may hold values from -6 to 6
- cholesky: float32 [512, 512], P(None, 'factors'), as said below
- reversion: float32 [512], P('factors'), may hold values from 0.05 to 2
- sabr_alpha: float32 [64], replicated, may hold values from 0.2 to 0.6
- sabr_rho: float32 [64], replicated, may hold values from -0.7 to 0.7
- sabr_nu: float32 [64], replicated, may hold values from 0.3 to 1.5
- factor_slice: int32 [512], P('factors'), may hold values from 0 to 63
- notional: float32 [32768], P('factors'), may hold values from -1 to 1
- strike: float32 [32768], P('factors'), may hold values from -3 to 3
- trade_set: int32 [32768], P('factors'), may hold values from 0 to 255
- trade_factor: int32 [32768], P('factors'), may hold values from 0 to 511, as said below
- loss_given: float32 [256], replicated, may hold values from 0.2 to 0.8
Outputs:
- path_adjoint: float32 [512, 2048], P('factors', 'paths')
- sabr_grad: float32 [3, 64], replicated
Inputs may be any that keep to these rules, and one draw needn't show every extreme that they name: `cholesky`: lower triangular with a positive diagonal and rows of unit length. `trade_factor`: trade t's factor lies in [(t // 4096) * 64, (t // 4096 + 1) * 64).
All inputs are finite; a program needn't handle non-finite values.
Results may differ from a plain program's by a relative error of at most 0.004.
Values may be sent and summed in bfloat16 or wider, within the bound.
A program may use at most 192 MiB of HBM per device.

v0:
```python
import math
import jax
import jax.numpy as jnp
from jax import lax
from jax.sharding import PartitionSpec as P

TIME_STEP = 0.25
ROOT_STEP = 0.5
DISCOUNT_RATE = 0.03
PRECISE = lax.Precision.HIGHEST
CONTRACT_FIRST = (((0,), (0,)), ((), ()))


def shortened(value):
    return jax.tree.map(lambda a: a.astype(jnp.bfloat16) if a.dtype == jnp.float32 else a, value)


def smile_terms(squashed, alpha_rows, rho_rows, nu_rows):
    curve = (2.0 - 3.0 * rho_rows * rho_rows) * nu_rows * nu_rows / 24.0
    base = 1.0 + 0.5 * rho_rows * nu_rows * squashed + curve * squashed * squashed
    rho_slope = alpha_rows * (
        0.5 * nu_rows * squashed - 0.25 * rho_rows * nu_rows * nu_rows * squashed * squashed
    )
    nu_slope = alpha_rows * (
        0.5 * rho_rows * squashed
        + (2.0 - 3.0 * rho_rows * rho_rows) * nu_rows * squashed * squashed / 12.0
    )
    level_slope = alpha_rows * (0.5 * rho_rows * nu_rows + 2.0 * curve * squashed)
    return (alpha_rows * base, base, rho_slope, nu_slope, level_slope)


def split_factors(
    x_start,
    shocks,
    cholesky,
    reversion,
    sabr_alpha,
    sabr_rho,
    sabr_nu,
    factor_slice,
    notional,
    strike,
    trade_set,
    trade_factor,
    loss_given,
):
    factor_rows, path_cols = x_start.shape
    step_count = shocks.shape[0]
    total_sets = loss_given.shape[0]
    factor_place = lax.axis_index("factors")
    slice_count = sabr_alpha.shape[0]
    slice_table = (
        factor_slice[:, None] == jnp.arange(slice_count, dtype=jnp.int32)[None, :]
    ).astype(jnp.float32)
    alpha_rows = jnp.dot(slice_table, sabr_alpha, precision=PRECISE)[:, None]
    rho_rows = jnp.dot(slice_table, sabr_rho, precision=PRECISE)[:, None]
    nu_rows = jnp.dot(slice_table, sabr_nu, precision=PRECISE)[:, None]
    local_factor = trade_factor - factor_place * factor_rows
    factor_table = (
        jnp.arange(factor_rows, dtype=jnp.int32)[:, None] == local_factor[None, :]
    ).astype(jnp.float32)
    set_table = (jnp.arange(total_sets, dtype=jnp.int32)[:, None] == trade_set[None, :]).astype(
        jnp.bfloat16
    )
    damping = (1.0 - reversion * TIME_STEP)[:, None]
    state = x_start
    states = [state]
    weights = []
    for step_index in range(step_count):
        squashed = jnp.tanh(state)
        local_vol = smile_terms(squashed, alpha_rows, rho_rows, nu_rows)[0]
        correlate_source = local_vol * shocks[step_index]
        mixed = lax.psum_scatter(
            jnp.dot(cholesky, correlate_source, precision=PRECISE),
            "factors",
            scatter_dimension=0,
            tiled=True,
        )
        state = damping * state + ROOT_STEP * mixed
        states.append(state)
        moneyness = jnp.take(state, local_factor, axis=0) - strike[:, None]
        values = (notional[:, None] * jnp.tanh(moneyness)).astype(jnp.bfloat16)
        discount = math.exp(-DISCOUNT_RATE * TIME_STEP * (step_index + 1))
        partial_sum = jnp.dot(set_table, values, preferred_element_type=jnp.float32)
        exposure = lax.psum(partial_sum.astype(jnp.bfloat16), "factors").astype(jnp.float32)
        weights.append(
            (discount * loss_given[:, None] * jax.nn.sigmoid(exposure)).astype(jnp.bfloat16)
        )
    adjoint = jnp.zeros_like(x_start)
    factor_sums = jnp.zeros((3, factor_rows), jnp.float32)
    for step_index in reversed(range(step_count)):
        moneyness = jnp.take(states[step_index + 1], local_factor, axis=0) - strike[:, None]
        squash_trade = jnp.tanh(moneyness)
        trade_term = (
            notional[:, None]
            * (1.0 - squash_trade * squash_trade)
            * lax.dot_general(
                set_table, weights[step_index], CONTRACT_FIRST, preferred_element_type=jnp.float32
            )
        )
        adjoint = adjoint + jnp.dot(factor_table, trade_term, precision=PRECISE)
        shock_adjoint = jnp.zeros((factor_rows, path_cols), jnp.float32) + lax.dot_general(
            cholesky,
            lax.all_gather(shortened(ROOT_STEP * adjoint), "factors", axis=0, tiled=True),
            CONTRACT_FIRST,
            precision=PRECISE,
        )
        squashed = jnp.tanh(states[step_index])
        local_vol, base, rho_slope, nu_slope, level_slope = smile_terms(
            squashed, alpha_rows, rho_rows, nu_rows
        )
        vol_adjoint = shock_adjoint * shocks[step_index]
        factor_sums = factor_sums + jnp.stack(
            [
                jnp.sum(vol_adjoint * base, axis=1),
                jnp.sum(vol_adjoint * rho_slope, axis=1),
                jnp.sum(vol_adjoint * nu_slope, axis=1),
            ]
        )
        adjoint = damping * adjoint + vol_adjoint * level_slope * (1.0 - squashed * squashed)
    slice_sums = jnp.dot(factor_sums, slice_table, precision=PRECISE)
    return (adjoint, slice_sums)


def per_device(
    x_start,
    shocks,
    cholesky,
    reversion,
    sabr_alpha,
    sabr_rho,
    sabr_nu,
    factor_slice,
    notional,
    strike,
    trade_set,
    trade_factor,
    loss_given,
):
    adjoint, slice_sums = split_factors(
        x_start,
        shocks,
        cholesky,
        reversion,
        sabr_alpha,
        sabr_rho,
        sabr_nu,
        factor_slice,
        notional,
        strike,
        trade_set,
        trade_factor,
        loss_given,
    )
    total_grad = lax.psum(slice_sums, ("paths", "factors"))
    sabr_grad = total_grad / (x_start.shape[1] * lax.axis_size("paths"))
    return (adjoint, sabr_grad)


def solution(mesh):
    return jax.shard_map(
        per_device,
        mesh=mesh,
        in_specs=(
            P("factors", "paths"),
            P(None, "factors", "paths"),
            P(None, "factors"),
            P("factors"),
            P(),
            P(),
            P(),
            P("factors"),
            P("factors"),
            P("factors"),
            P("factors"),
            P("factors"),
            P(),
        ),
        out_specs=(P("factors", "paths"), P()),
        check_vma=False,
    )
```

profile of v0, /device:TPU:0, one launch (start us, length us, event | category | flops | bytes accessed | tf_op | source)
XLA Modules:
  0.0 588.1 jit_solution(14679514657513539477)
XLA Ops:
  7.2 0.9 convolution_bitcast_fusion.9
  8.2 0.9 convolution_bitcast_fusion.10
  9.1 0.9 broadcast_multiply_fusion.5
  10.0 2.1 convolution_bitcast_fusion.3
  12.1 1.3 copy.39
  13.5 0.7 multiply_subtract_fusion
  14.2 66.8 %reduce-scatter.13.cloned.1.call-done = f32[64,512]{1,0:T(8,128)} async-done(((f32[512,512]{1,0:T(8,128)}), f32[64,512]{1,0:T(8,128)}) %reduce-scatter.13.cloned.1.call-update) | async-done | bytes 131088 | tf_op jit(solution)/shard_map/reduce_scatter | solution.py:73
  80.9 1.0 multiply_add_fusion.4
  82.0 2.0 convolution_bitcast_fusion.2
  84.0 1.3 copy.41
  85.4 63.6 %reduce-scatter.15.cloned.1.call-done = f32[64,512]{1,0:T(8,128)} async-done(((f32[512,512]{1,0:T(8,128)}), f32[64,512]{1,0:T(8,128)}) %reduce-scatter.15.cloned.1.call-update) | async-done | bytes 131088 | tf_op jit(solution)/shard_map/reduce_scatter | solution.py:73
  149.0 1.0 multiply_add_fusion.3
  150.0 1.1 convolution_bitcast_fusion.1
  151.1 1.4 copy.43
  152.7 16.8 %gather_fusion.3 = f32[4096,512]{1,0:T(8,128)} fusion(f32[64,512]{1,0:T(8,128)S(1)} %multiply_add_fusion.4, s32[4096]{0:T(1024)S(1)} %fusion.166), kind=kCustom, calls=%fused_computation.3.clone | custom fusion | bytes 16793600 | tf_op jit(solution)/shard_map/jit(_take)/gather | solution.py:92
  169.5 46.4 %reduce-scatter.17.cloned.1.call-done = f32[64,512]{1,0:T(8,128)} async-done(((f32[512,512]{1,0:T(8,128)}), f32[64,512]{1,0:T(8,128)}) %reduce-scatter.17.cloned.1.call-update) | async-done | bytes 131088 | tf_op jit(solution)/shard_map/reduce_scatter | solution.py:73
  215.9 1.0 multiply_add_fusion.2
  216.8 1.1 convolution_bitcast_fusion
  218.0 1.4 copy.45
  219.8 6.3 %fusion.67 = bf16[256,512]{1,0:T(8,128)(2,1)} fusion(f32[4096,512]{1,0:T(8,128)} %gather_fusion.3, f32[4096]{0:T(1024)S(1)} %copy-done.10, f32[4096]{0:T(1024)S(1)} %copy-done.11, pred[4096]{0:T(1024)(128)(4,1)S(1)} %get-tuple-element.32, s32[4096]{0:T(1024)S(1)} %copy-done.3), kind=kOutput, calls=%fused_computation.80 | convolution fusion | flops 1083310080 | bytes 8704000 | tf_op jit(solution)/shard_map/dot_general | solution.py:84
  226.1 16.8 %gather_fusion.2 = f32[4096,512]{1,0:T(8,128)} fusion(f32[64,512]{1,0:T(8,128)S(1)} %multiply_add_fusion.3, s32[4096]{0:T(1024)S(1)} %fusion.166), kind=kCustom, calls=%fused_computation.2.clone | custom fusion | bytes 16793600 | tf_op jit(solution)/shard_map/jit(_take)/gather | solution.py:92
  242.9 6.3 %fusion.66 = bf16[256,512]{1,0:T(8,128)(2,1)} fusion(f32[4096,512]{1,0:T(8,128)} %gather_fusion.2, f32[4096]{0:T(1024)S(1)} %copy-done.10, f32[4096]{0:T(1024)S(1)} %copy-done.11, pred[4096]{0:T(1024)(128)(4,1)S(1)} %get-tuple-element.32, s32[4096]{0:T(1024)S(1)} %copy-done.3), kind=kOutput, calls=%fused_computation.79 | convolution fusion | flops 1083310080 | bytes 8704000 | tf_op jit(solution)/shard_map/dot_general | solution.py:84
  249.2 16.8 %gather_fusion.1 = f32[4096,512]{1,0:T(8,128)} fusion(f32[64,512]{1,0:T(8,128)S(1)} %multiply_add_fusion.2, s32[4096]{0:T(1024)S(1)} %fusion.166), kind=kCustom, calls=%fused_computation.1.clone | custom fusion | bytes 16793600 | tf_op jit(solution)/shard_map/jit(_take)/gather | solution.py:92
  266.0 6.4 %fusion.65 = bf16[256,512]{1,0:T(8,128)(2,1)} fusion(f32[4096,512]{1,0:T(8,128)} %gather_fusion.1, f32[4096]{0:T(1024)S(1)} %copy-done.10, f32[4096]{0:T(1024)S(1)} %copy-done.11, pred[4096]{0:T(1024)(128)(4,1)S(1)} %get-tuple-element.32, s32[4096]{0:T(1024)S(1)} %copy-done.3), kind=kOutput, calls=%fused_computation.78 | convolution fusion | flops 1083310080 | bytes 8704000 | tf_op jit(solution)/shard_map/dot_general | solution.py:84
  272.3 10.4 %reduce-scatter.19.cloned.1.call-done = f32[64,512]{1,0:T(8,128)} async-done(((f32[512,512]{1,0:T(8,128)}), f32[64,512]{1,0:T(8,128)}) %reduce-scatter.19.cloned.1.call-update) | async-done | bytes 131088 | tf_op jit(solution)/shard_map/reduce_scatter | solution.py:73
  282.7 1.0 multiply_add_fusion.1
  283.7 16.8 %gather_fusion = f32[4096,512]{1,0:T(8,128)} fusion(f32[64,512]{1,0:T(8,128)S(1)} %multiply_add_fusion.1, s32[4096]{0:T(1024)S(1)} %fusion.166), kind=kCustom, calls=%fused_computation.clone | custom fusion | bytes 16793600 | tf_op jit(solution)/shard_map/jit(_take)/gather | solution.py:92
  300.5 6.3 %fusion.64 = bf16[256,512]{1,0:T(8,128)(2,1)} fusion(f32[4096,512]{1,0:T(8,128)} %gather_fusion, f32[4096]{0:T(1024)S(1)} %copy-done.10, f32[4096]{0:T(1024)S(1)} %copy-done.11, pred[4096]{0:T(1024)(128)(4,1)S(1)} %get-tuple-element.32, s32[4096]{0:T(1024)S(1)} %copy-done.3), kind=kOutput, calls=%fused_computation.77 | convolution fusion | flops 1083310080 | bytes 8704000 | tf_op jit(solution)/shard_map/dot_general | solution.py:84
  306.9 77.6 %all-reduce.3.cloned.1.call-done = (bf16[256,512]{1,0:T(8,128)(2,1)}, bf16[256,512]{1,0:T(8,128)(2,1)}, bf16[256,512]{1,0:T(8,128)(2,1)}, bf16[256,512]{1,0:T(8,128)(2,1)}) async-done(((bf16[256,512]{1,0:T(8,128)(2,1)}, bf16[256,512]{1,0:T(8,128)(2,1)}, bf16[256,512]{1,0:T(8,128)(2,1)}, bf16[256,512]{1,0:T(8,128)(2,1)}), (bf16[256,512]{1,0:T(8,128)(2,1)}, bf16[256,512]{1,0:T(8,128)(2,1)}, ...) | async-done | bytes 1048592 | tf_op jit(solution)/shard_map/psum | solution.py:85
  384.5 2.5 fusion.38
  387.0 1.0 copy-done.1
  387.9 5.4 multiply_convert_fusion.27
  393.3 31.8 %all_gather.12 = bf16[512,512]{1,0:T(8,128)(2,1)S(1)} all-gather(bf16[64,512]{1,0:T(8,128)(2,1)S(1)} %get-tuple-element.45), channel_id=1, replica_groups=mesh['paths'=4,'factors'=8] {'factors'}, dimensions={0}, use_global_device_ids=true | all-gather | bytes 589824 | tf_op jit(solution)/shard_map/all_gather | solution.py:104
  425.1 0.4 fusion.71
  425.5 1.4 fusion.36
  427.0 5.4 multiply_convert_fusion.26
  432.3 31.6 %all_gather.13 = bf16[512,512]{1,0:T(8,128)(2,1)S(1)} all-gather(bf16[64,512]{1,0:T(8,128)(2,1)S(1)} %get-tuple-element.47), channel_id=1, replica_groups=mesh['paths'=4,'factors'=8] {'factors'}, dimensions={0}, use_global_device_ids=true | all-gather | bytes 589824 | tf_op jit(solution)/shard_map/all_gather | solution.py:104
  463.9 0.4 fusion.70
  464.3 1.4 fusion.34
  465.8 5.4 multiply_convert_fusion.25
  471.2 31.5 %all_gather.14 = bf16[512,512]{1,0:T(8,128)(2,1)S(1)} all-gather(bf16[64,512]{1,0:T(8,128)(2,1)S(1)} %get-tuple-element.49), channel_id=1, replica_groups=mesh['paths'=4,'factors'=8] {'factors'}, dimensions={0}, use_global_device_ids=true | all-gather | bytes 589824 | tf_op jit(solution)/shard_map/all_gather | solution.py:104
  502.7 0.4 fusion.69
  503.1 1.4 fusion.32
  504.5 5.4 multiply_convert_fusion.24
  509.9 31.2 %all_gather.15 = bf16[512,512]{1,0:T(8,128)(2,1)S(1)} all-gather(bf16[64,512]{1,0:T(8,128)(2,1)S(1)} %get-tuple-element.51), channel_id=1, replica_groups=mesh['paths'=4,'factors'=8] {'factors'}, dimensions={0}, use_global_device_ids=true | all-gather | bytes 589824 | tf_op jit(solution)/shard_map/all_gather | solution.py:104
  541.1 1.6 fusion.100
  542.9 37.8 %psum.39 = f32[3,64]{1,0:T(4,128)S(1)} all-reduce(f32[3,64]{1,0:T(4,128)S(1)} %fusion.161), channel_id=1, replica_groups=mesh['paths'=4,'factors'=8] {'paths','factors'}, use_global_device_ids=true, to_apply=%region_20.22 | all-reduce | flops 192 | bytes 1536 | tf_op jit(solution)/shard_map/psum | solution.py:155
  580.8 0.6 broadcast_multiply_fusion
  (55 shorter events, 0.9 us)
Async XLA Ops:
  7.2 2.8 copy-start
  7.2 142.8 %copy-start.2 = (f32[4,64,512]{2,1,0:T(8,128)S(1)}, f32[4,64,512]{2,1,0:T(8,128)}, u32[]{:S(2)}) copy-start(f32[4,64,512]{2,1,0:T(8,128)} %param.16) | copy-start | bytes 1572868
  7.2 145.4 %copy-start.8 = (s32[4096]{0:T(1024)S(1)}, s32[4096]{0:T(1024)}, u32[]{:S(2)}) copy-start(s32[4096]{0:T(1024)} %param.26) | copy-start | bytes 49156
  7.2 73.7 %reduce-scatter.13.cloned.1.call-start = ((), (), s32[]{:S(2)}) async-start(), calls=%async_computation.4 | async-start | bytes 1179648 | tf_op jit(solution)/shard_map/reduce_scatter | solution.py:73
  13.5 135.6 %reduce-scatter.15.cloned.1.call-start = ((), (), s32[]{:S(2)}) async-start(), calls=%async_computation.5 | async-start | bytes 1179648 | tf_op jit(solution)/shard_map/reduce_scatter | solution.py:73
  85.4 130.5 %reduce-scatter.17.cloned.1.call-start = ((), (), s32[]{:S(2)}) async-start(), calls=%async_computation.6 | async-start | bytes 1179648 | tf_op jit(solution)/shard_map/reduce_scatter | solution.py:73
  152.6 130.2 %reduce-scatter.19.cloned.1.call-start = ((), (), s32[]{:S(2)}) async-start(), calls=%async_computation.7 | async-start | bytes 1179648 | tf_op jit(solution)/shard_map/reduce_scatter | solution.py:73
  152.7 67.1 %copy-start.3 = (s32[4096]{0:T(1024)S(1)}, s32[4096]{0:T(1024)}, u32[]{:S(2)}) copy-start(s32[4096]{0:T(1024)} %param.25) | copy-start | bytes 49156
  152.7 67.1 %copy-start.10 = (f32[4096]{0:T(1024)S(1)}, f32[4096]{0:T(1024)}, u32[]{:S(2)}) copy-start(f32[4096]{0:T(1024)} %param.24) | copy-start | bytes 49156
  152.7 67.1 %copy-start.11 = (f32[4096]{0:T(1024)S(1)}, f32[4096]{0:T(1024)}, u32[]{:S(2)}) copy-start(f32[4096]{0:T(1024)} %param.23) | copy-start | bytes 49156
  219.4 165.1 %all-reduce.3.cloned.1.call-start = ((), (), s32[]{:S(2)}) async-start(), calls=%async_computation.8 | async-start | bytes 2097152 | tf_op jit(solution)/shard_map/psum | solution.py:85
  300.5 6.4 %copy-start.9 = (f32[256]{0:T(256)S(1)}, f32[256]{0:T(256)}, u32[]{:S(2)}) copy-start(f32[256]{0:T(256)} %param.27) | copy-start | bytes 3076
  384.5 3.5 copy-start.1
  384.5 42.4 %slice-start.4 = ((s8[8388608]{0:T(1024)(128)(4,1)}), s8[4194304]{0:T(1024)(128)(4,1)S(1)}, s32[]{:S(2)}) async-start(s8[8388608]{0:T(1024)(128)(4,1)} %bitcast.89), calls=%async_computation.13 | async-start | bytes 8388608
  387.9 37.6 %copy-start.7 = (bf16[256,512]{1,0:T(8,128)(2,1)S(1)}, bf16[256,512]{1,0:T(8,128)(2,1)}, u32[]{:S(2)}) copy-start(bf16[256,512]{1,0:T(8,128)(2,1)} %get-tuple-element.28) | copy-start | bytes 786436
  387.9 39.0 %slice-start.5 = ((s8[8388608]{0:T(1024)(128)(4,1)}), s8[4194304]{0:T(1024)(128)(4,1)S(1)}, s32[]{:S(2)}) async-start(s8[8388608]{0:T(1024)(128)(4,1)} %bitcast.89), calls=%async_computation.14 | async-start | bytes 8388608
  426.9 38.8 %slice-start.2 = ((s8[8388608]{0:T(1024)(128)(4,1)}), s8[4194304]{0:T(1024)(128)(4,1)S(1)}, s32[]{:S(2)}) async-start(s8[8388608]{0:T(1024)(128)(4,1)} %bitcast.87), calls=%async_computation.11 | async-start | bytes 8388608
  427.0 37.4 %copy-start.6 = (bf16[256,512]{1,0:T(8,128)(2,1)S(1)}, bf16[256,512]{1,0:T(8,128)(2,1)}, u32[]{:S(2)}) copy-start(bf16[256,512]{1,0:T(8,128)(2,1)} %get-tuple-element.27) | copy-start | bytes 786436
  427.0 38.8 %slice-start.3 = ((s8[8388608]{0:T(1024)(128)(4,1)}), s8[4194304]{0:T(1024)(128)(4,1)S(1)}, s32[]{:S(2)}) async-start(s8[8388608]{0:T(1024)(128)(4,1)} %bitcast.87), calls=%async_computation.12 | async-start | bytes 8388608
  465.7 38.7 %slice-start = ((s8[8388608]{0:T(1024)(128)(4,1)}), s8[4194304]{0:T(1024)(128)(4,1)S(1)}, s32[]{:S(2)}) async-start(s8[8388608]{0:T(1024)(128)(4,1)} %bitcast.85), calls=%async_computation.9 | async-start | bytes 8388608
  465.8 37.3 %copy-start.5 = (bf16[256,512]{1,0:T(8,128)(2,1)S(1)}, bf16[256,512]{1,0:T(8,128)(2,1)}, u32[]{:S(2)}) copy-start(bf16[256,512]{1,0:T(8,128)(2,1)} %get-tuple-element.26) | copy-start | bytes 786436
  465.8 38.7 %slice-start.1 = ((s8[8388608]{0:T(1024)(128)(4,1)}), s8[4194304]{0:T(1024)(128)(4,1)S(1)}, s32[]{:S(2)}) async-start(s8[8388608]{0:T(1024)(128)(4,1)} %bitcast.85), calls=%async_computation.10 | async-start | bytes 8388608
  504.5 36.6 %copy-start.4 = (f32[64,512]{1,0:T(8,128)S(1)}, f32[64,512]{1,0:T(8,128)}, u32[]{:S(2)}) copy-start(f32[64,512]{1,0:T(8,128)} %param.15) | copy-start | bytes 393220
  504.5 38.2 %copy-start.12 = (s32[64]{0:T(128)S(1)}, s32[64]{0:T(128)}, u32[]{:S(2)}) copy-start(s32[64]{0:T(128)} %param.22) | copy-start | bytes 772
Sparse Core Ops, SparseCore 0:
  13.6 67.3 reduce-scatter.12
  85.5 63.4 reduce-scatter.14
  152.7 63.1 reduce-scatter.16
  219.5 63.1 reduce-scatter.18
  307.0 77.4 all-reduce.2
where the time goes:
time: 593 us; the launch traced here: 588 us
  waiting for transfers between devices  265 us (45%)
  blocking collectives  164 us (28%)
  local copies, waits for them, and re-layouts  73.7 us (12%)
  matrix products  65.5 us (11%)
  between operations  14.4 us (2%)
    reduce_scatter x4, waiting for transfers between devices, split_factors(): lax.psum_scatter(jnp.dot(cholesky, correlate_source, precision=PRECISE),...  187 us
    all_gather x4, blocking collectives, split_factors(): lax.all_gather(shortened(ROOT_STEP * adjoint), 'factors', axis=0, tiled=T...  126 us
    psum x1, waiting for transfers between devices, split_factors(): lax.psum(partial_sum.astype(jnp.bfloat16), 'factors').astype(jnp.float32)  77.6 us
    gather x4, local copies, waits for them, and re-layouts, split_factors(): jnp.take(states[step_index + 1], local_factor, axis=0) - strike[:, None]  67.2 us
    psum x1, blocking collectives, per_device(): total_grad = lax.psum(slice_sums, ('paths', 'factors'))  37.8 us
    dot_general x4, matrix products, split_factors(): partial_sum = jnp.dot(set_table, values, preferred_element_type=jnp.float32)  25.3 us
    dot_general x4, matrix products, split_factors(): adjoint = adjoint + jnp.dot(factor_table, trade_term, precision=PRECISE)  21.5 us
  transfers between devices with their start and end apart: 5, of which 5 were waited for; matrix products, arithmetic and copies ran while one was open for 12% of the time, Pallas kernels for 0%

commit v1 on v0

--- a/solution.py
+++ b/solution.py
@@ -9,6 +9,18 @@
 DISCOUNT_RATE = 0.03
 PRECISE = lax.Precision.HIGHEST
 CONTRACT_FIRST = (((0,), (0,)), ((), ()))
+
+
+def collect(value, axis, dim):
+    ways, here = (lax.axis_size(axis), lax.axis_index(axis))
+    grown, reach = (value, 1)
+    while reach < ways:
+        theirs = lax.ppermute(grown, axis, [(d, d ^ reach) for d in range(ways)])
+        mine_first = jnp.concatenate([grown, theirs], axis=dim)
+        theirs_first = jnp.concatenate([theirs, grown], axis=dim)
+        grown = jnp.where(here & reach == 0, mine_first, theirs_first)
+        reach = 2 * reach
+    return grown
 
 
 def shortened(value):
@@ -101,7 +113,7 @@
         adjoint = adjoint + jnp.dot(factor_table, trade_term, precision=PRECISE)
         shock_adjoint = jnp.zeros((factor_rows, path_cols), jnp.float32) + lax.dot_general(
             cholesky,
-            lax.all_gather(shortened(ROOT_STEP * adjoint), "factors", axis=0, tiled=True),
+            collect(shortened(ROOT_STEP * adjoint), "factors", 0),
             CONTRACT_FIRST,
             precision=PRECISE,
         )

time: 593 us -> 555 us (0.936)
  blocking collectives: 164 us -> 38.4 us
  waiting for transfers between devices: 265 us -> 333 us
  starting transfers between devices: 0.5 us -> 10.5 us
  matrix products: 65.5 us -> 72.1 us
    all_gather x4 -> x0, blocking collectives: 126 us -> none  [split_factors(): lax.all_gather(shortened(ROOT_STEP * adjoint), 'factors', axis=0, tiled=T...]
    ppermute x0 -> x12, waiting for transfers between devices: none -> 68.3 us  [collect(): theirs = lax.ppermute(grown, axis, [(d, d ^ reach) for d in range(ways)])]
    ppermute x0 -> x12, starting transfers between devices: none -> 10.3 us  [collect(): theirs = lax.ppermute(grown, axis, [(d, d ^ reach) for d in range(ways)])]
    dot_general x4, matrix products: 21.5 us -> 27.4 us  [split_factors(): adjoint = adjoint + jnp.dot(factor_table, trade_term, precision=PRECISE)]
  transfers between devices with their start and end apart: 5 -> 17, of which waited for: 5 -> 17; matrix products, arithmetic and copies ran while one was open for 12% -> 14% of each run, Pallas kernels for 0% -> 0%
where the time goes in v1:
time: 555 us; the launch traced here: 547 us
  waiting for transfers between devices  333 us (60%)
  local copies, waits for them, and re-layouts  73.5 us (13%)
  matrix products  72.1 us (13%)
  blocking collectives  38.4 us (7%)
  between operations  14.4 us (3%)
  starting transfers between devices  10.5 us (2%)
  other arithmetic  5.61 us (1%)
    reduce_scatter x4, waiting for transfers between devices, split_factors(): lax.psum_scatter(jnp.dot(cholesky, correlate_source, precision=PRECISE),...  187 us
    psum x1, waiting for transfers between devices, split_factors(): lax.psum(partial_sum.astype(jnp.bfloat16), 'factors').astype(jnp.float32)  77.5 us
    ppermute x12, waiting for transfers between devices, collect(): theirs = lax.ppermute(grown, axis, [(d, d ^ reach) for d in range(ways)])  68.3 us
    gather x4, local copies, waits for them, and re-layouts, split_factors(): jnp.take(states[step_index + 1], local_factor, axis=0) - strike[:, None]  67.1 us
    psum x1, blocking collectives, per_device(): total_grad = lax.psum(slice_sums, ('paths', 'factors'))  38.4 us
    dot_general x4, matrix products, split_factors(): adjoint = adjoint + jnp.dot(factor_table, trade_term, precision=PRECISE)  27.4 us
    dot_general x4, matrix products, split_factors(): partial_sum = jnp.dot(set_table, values, preferred_element_type=jnp.float32)  25.8 us
  transfers between devices with their start and end apart: 17, of which 17 were waited for; matrix products, arithmetic and copies ran while one was open for 14% of the time, Pallas kernels for 0%

profile of v1, /device:TPU:0, one launch (start us, length us, event | category | flops | bytes accessed | tf_op | source)
XLA Modules:
  0.0 547.0 jit_solution(869553075853794082)
XLA Ops:
  10.0 2.1 convolution_bitcast_fusion.3
  12.1 1.3 copy.39
  14.1 66.4 %reduce-scatter.13.cloned.1.call-done = f32[64,512]{1,0:T(8,128)} async-done(((f32[512,512]{1,0:T(8,128)}), f32[64,512]{1,0:T(8,128)}) %reduce-scatter.13.cloned.1.call-update) | async-done | bytes 131088 | tf_op jit(solution)/shard_map/reduce_scatter | solution.py:85
  81.6 2.0 convolution_bitcast_fusion.2
  83.6 1.3 copy.41
  85.0 63.2 %reduce-scatter.15.cloned.1.call-done = f32[64,512]{1,0:T(8,128)} async-done(((f32[512,512]{1,0:T(8,128)}), f32[64,512]{1,0:T(8,128)}) %reduce-scatter.15.cloned.1.call-update) | async-done | bytes 131088 | tf_op jit(solution)/shard_map/reduce_scatter | solution.py:85
  149.2 1.1 convolution_bitcast_fusion.1
  150.4 1.4 copy.43
  151.9 16.8 %gather_fusion.3 = f32[4096,512]{1,0:T(8,128)} fusion(f32[64,512]{1,0:T(8,128)S(1)} %multiply_add_fusion.4, s32[4096]{0:T(1024)S(1)} %fusion.190), kind=kCustom, calls=%fused_computation.3.clone | custom fusion | bytes 16793600 | tf_op jit(solution)/shard_map/jit(_take)/gather | solution.py:104
  168.7 46.4 %reduce-scatter.17.cloned.1.call-done = f32[64,512]{1,0:T(8,128)} async-done(((f32[512,512]{1,0:T(8,128)}), f32[64,512]{1,0:T(8,128)}) %reduce-scatter.17.cloned.1.call-update) | async-done | bytes 131088 | tf_op jit(solution)/shard_map/reduce_scatter | solution.py:85
  217.2 1.4 copy.45
  218.7 6.3 %fusion.67 = bf16[256,512]{1,0:T(8,128)(2,1)} fusion(f32[4096,512]{1,0:T(8,128)} %gather_fusion.3, f32[4096]{0:T(1024)S(1)} %copy-done.10, f32[4096]{0:T(1024)S(1)} %copy-done.11, pred[4096]{0:T(1024)(128)(4,1)S(1)} %get-tuple-element.32, s32[4096]{0:T(1024)S(1)} %copy-done.2), kind=kOutput, calls=%fused_computation.80 | convolution fusion | flops 1083310080 | bytes 8704000 | tf_op jit(solution)/shard_map/dot_general | solution.py:96
  225.0 16.8 %gather_fusion.2 = f32[4096,512]{1,0:T(8,128)} fusion(f32[64,512]{1,0:T(8,128)S(1)} %multiply_add_fusion.3, s32[4096]{0:T(1024)S(1)} %fusion.190), kind=kCustom, calls=%fused_computation.2.clone | custom fusion | bytes 16793600 | tf_op jit(solution)/shard_map/jit(_take)/gather | solution.py:104
  241.8 6.3 %fusion.66 = bf16[256,512]{1,0:T(8,128)(2,1)} fusion(f32[4096,512]{1,0:T(8,128)} %gather_fusion.2, f32[4096]{0:T(1024)S(1)} %copy-done.10, f32[4096]{0:T(1024)S(1)} %copy-done.11, pred[4096]{0:T(1024)(128)(4,1)S(1)} %get-tuple-element.32, s32[4096]{0:T(1024)S(1)} %copy-done.2), kind=kOutput, calls=%fused_computation.79 | convolution fusion | flops 1083310080 | bytes 8704000 | tf_op jit(solution)/shard_map/dot_general | solution.py:96
  248.1 16.8 %gather_fusion.1 = f32[4096,512]{1,0:T(8,128)} fusion(f32[64,512]{1,0:T(8,128)S(1)} %multiply_add_fusion.2, s32[4096]{0:T(1024)S(1)} %fusion.190), kind=kCustom, calls=%fused_computation.1.clone | custom fusion | bytes 16793600 | tf_op jit(solution)/shard_map/jit(_take)/gather | solution.py:104
  264.9 6.4 %fusion.65 = bf16[256,512]{1,0:T(8,128)(2,1)} fusion(f32[4096,512]{1,0:T(8,128)} %gather_fusion.1, f32[4096]{0:T(1024)S(1)} %copy-done.10, f32[4096]{0:T(1024)S(1)} %copy-done.11, pred[4096]{0:T(1024)(128)(4,1)S(1)} %get-tuple-element.32, s32[4096]{0:T(1024)S(1)} %copy-done.2), kind=kOutput, calls=%fused_computation.78 | convolution fusion | flops 1083310080 | bytes 8704000 | tf_op jit(solution)/shard_map/dot_general | solution.py:96
  271.3 10.6 %reduce-scatter.19.cloned.1.call-done = f32[64,512]{1,0:T(8,128)} async-done(((f32[512,512]{1,0:T(8,128)}), f32[64,512]{1,0:T(8,128)}) %reduce-scatter.19.cloned.1.call-update) | async-done | bytes 131088 | tf_op jit(solution)/shard_map/reduce_scatter | solution.py:85
  282.8 16.8 %gather_fusion = f32[4096,512]{1,0:T(8,128)} fusion(f32[64,512]{1,0:T(8,128)S(1)} %multiply_add_fusion.1, s32[4096]{0:T(1024)S(1)} %fusion.190), kind=kCustom, calls=%fused_computation.clone | custom fusion | bytes 16793600 | tf_op jit(solution)/shard_map/jit(_take)/gather | solution.py:104
  299.6 6.8 %fusion.64 = bf16[256,512]{1,0:T(8,128)(2,1)} fusion(f32[4096,512]{1,0:T(8,128)} %gather_fusion, f32[4096]{0:T(1024)S(1)} %copy-done.10, f32[4096]{0:T(1024)S(1)} %copy-done.11, pred[4096]{0:T(1024)(128)(4,1)S(1)} %get-tuple-element.32, s32[4096]{0:T(1024)S(1)} %copy-done.2), kind=kOutput, calls=%fused_computation.77 | convolution fusion | flops 1083310080 | bytes 8704000 | tf_op jit(solution)/shard_map/dot_general | solution.py:96
  306.4 77.5 %all-reduce.3.cloned.1.call-done = (bf16[256,512]{1,0:T(8,128)(2,1)}, bf16[256,512]{1,0:T(8,128)(2,1)}, bf16[256,512]{1,0:T(8,128)(2,1)}, bf16[256,512]{1,0:T(8,128)(2,1)}) async-done(((bf16[256,512]{1,0:T(8,128)(2,1)}, bf16[256,512]{1,0:T(8,128)(2,1)}, bf16[256,512]{1,0:T(8,128)(2,1)}, bf16[256,512]{1,0:T(8,128)(2,1)}), (bf16[256,512]{1,0:T(8,128)(2,1)}, bf16[256,512]{1,0:T(8,128)(2,1)}, ...) | async-done | bytes 1048592 | tf_op jit(solution)/shard_map/psum | solution.py:97
  383.9 2.5 fusion.38
  387.4 5.4 multiply_convert_fusion.27
  392.8 1.5 collective-permute-start
  394.3 2.8 collective-permute-done
  397.1 1.2 collective-permute-start.1
  398.3 3.8 collective-permute-done.1
  402.2 1.3 collective-permute-start.2
  403.6 1.4 fusion.36
  405.0 9.0 %collective-permute-done.2 = bf16[256,512]{1,0:T(8,128)(2,1)S(1)} collective-permute-done((bf16[256,512]{1,0:T(8,128)(2,1)S(1)}, bf16[256,512]{1,0:T(8,128)(2,1)S(1)}, u32[]{:S(2)}, u32[]{:S(2)}) %collective-permute-start.2) | collective-permute-done | bytes 262176 | tf_op jit(solution)/shard_map/ppermute | solution.py:18
  414.4 11.1 %multiply_convert_fusion.26 = (bf16[64,512]{1,0:T(8,128)(2,1)S(1)}, f32[64,512]{1,0:T(8,128)S(1)}) fusion(f32[4096,512]{1,0:T(8,128)S(1)} %fusion.36, f32[4096,512]{1,0:T(8,128)} %gather_fusion.1, f32[4096]{0:T(1024)S(1)} %copy-done.10, f32[4096]{0:T(1024)S(1)} %copy-done.11, pred[4096]{0:T(1024)(128)(4,1)S(1)} %get-tuple-element.32, ...), kind=kOutput, calls=%fused_computation.211 | convolution fusion | flops 1623851008 | bytes 17421312 | tf_op jit(solution)/shard_map/dot_general | solution.py:113
  425.5 1.8 collective-permute-start.3
  427.3 2.5 collective-permute-done.3
  430.0 5.0 collective-permute-done.4
  435.3 1.4 fusion.34
  436.7 9.7 %collective-permute-done.5 = bf16[256,512]{1,0:T(8,128)(2,1)S(1)} collective-permute-done((bf16[256,512]{1,0:T(8,128)(2,1)S(1)}, bf16[256,512]{1,0:T(8,128)(2,1)S(1)}, u32[]{:S(2)}, u32[]{:S(2)}) %collective-permute-start.5) | collective-permute-done | bytes 262176 | tf_op jit(solution)/shard_map/ppermute | solution.py:18
  446.9 5.4 multiply_convert_fusion.25
  452.3 1.8 collective-permute-start.6
  454.1 2.5 collective-permute-done.6
  456.7 5.0 collective-permute-done.7
  461.9 1.4 fusion.32
  463.3 9.7 %collective-permute-done.8 = bf16[256,512]{1,0:T(8,128)(2,1)S(1)} collective-permute-done((bf16[256,512]{1,0:T(8,128)(2,1)S(1)}, bf16[256,512]{1,0:T(8,128)(2,1)S(1)}, u32[]{:S(2)}, u32[]{:S(2)}) %collective-permute-start.8) | collective-permute-done | bytes 262176 | tf_op jit(solution)/shard_map/ppermute | solution.py:18
  473.5 5.6 %multiply_convert_fusion.24 = (bf16[64,512]{1,0:T(8,128)(2,1)S(1)}, f32[64,512]{1,0:T(8,128)S(1)}) fusion(f32[4096,512]{1,0:T(8,128)S(1)} %fusion.32, f32[4096,512]{1,0:T(8,128)S(1)} %bitcast.82, f32[4096]{0:T(1024)S(1)} %copy-done.10, f32[4096]{0:T(1024)S(1)} %copy-done.11, pred[4096]{0:T(1024)(128)(4,1)S(1)} %get-tuple-element.32, ...), kind=kOutput, calls=%fused_computation.209 | convolution fusion | flops 1623851008 | bytes 17421312 | tf_op jit(solution)/shard_map/dot_general | solution.py:113
  479.1 1.8 collective-permute-start.9
  480.9 2.5 collective-permute-done.9
  483.5 5.0 collective-permute-done.10
  488.7 10.7 %collective-permute-done.11 = bf16[256,512]{1,0:T(8,128)(2,1)S(1)} collective-permute-done((bf16[256,512]{1,0:T(8,128)(2,1)S(1)}, bf16[256,512]{1,0:T(8,128)(2,1)S(1)}, u32[]{:S(2)}, u32[]{:S(2)}) %collective-permute-start.11) | collective-permute-done | bytes 262176 | tf_op jit(solution)/shard_map/ppermute | solution.py:18
  499.4 1.7 fusion.124
  501.3 38.4 %psum.39 = f32[3,64]{1,0:T(4,128)S(1)} all-reduce(f32[3,64]{1,0:T(4,128)S(1)} %fusion.185), channel_id=1, replica_groups=mesh['paths'=4,'factors'=8] {'paths','factors'}, use_global_device_ids=true, to_apply=%region_20.22 | all-reduce | flops 192 | bytes 1536 | tf_op jit(solution)/shard_map/psum | solution.py:167
  (78 shorter events, 13.2 us)
Async XLA Ops:
  7.2 2.8 copy-start
  7.2 142.0 %copy-start.3 = (f32[4,64,512]{2,1,0:T(8,128)S(1)}, f32[4,64,512]{2,1,0:T(8,128)}, u32[]{:S(2)}) copy-start(f32[4,64,512]{2,1,0:T(8,128)} %param.16) | copy-start | bytes 1572868
  7.2 144.6 %copy-start.8 = (s32[4096]{0:T(1024)S(1)}, s32[4096]{0:T(1024)}, u32[]{:S(2)}) copy-start(s32[4096]{0:T(1024)} %param.26) | copy-start | bytes 49156
  7.2 73.4 %reduce-scatter.13.cloned.1.call-start = ((), (), s32[]{:S(2)}) async-start(), calls=%async_computation.4 | async-start | bytes 1179648 | tf_op jit(solution)/shard_map/reduce_scatter | solution.py:85
  13.4 134.8 %reduce-scatter.15.cloned.1.call-start = ((), (), s32[]{:S(2)}) async-start(), calls=%async_computation.5 | async-start | bytes 1179648 | tf_op jit(solution)/shard_map/reduce_scatter | solution.py:85
  85.0 130.1 %reduce-scatter.17.cloned.1.call-start = ((), (), s32[]{:S(2)}) async-start(), calls=%async_computation.6 | async-start | bytes 1179648 | tf_op jit(solution)/shard_map/reduce_scatter | solution.py:85
  151.8 130.1 %reduce-scatter.19.cloned.1.call-start = ((), (), s32[]{:S(2)}) async-start(), calls=%async_computation.7 | async-start | bytes 1179648 | tf_op jit(solution)/shard_map/reduce_scatter | solution.py:85
  151.8 66.8 %copy-start.2 = (s32[4096]{0:T(1024)S(1)}, s32[4096]{0:T(1024)}, u32[]{:S(2)}) copy-start(s32[4096]{0:T(1024)} %param.25) | copy-start | bytes 49156
  151.9 66.8 %copy-start.10 = (f32[4096]{0:T(1024)S(1)}, f32[4096]{0:T(1024)}, u32[]{:S(2)}) copy-start(f32[4096]{0:T(1024)} %param.24) | copy-start | bytes 49156
  151.9 66.8 %copy-start.11 = (f32[4096]{0:T(1024)S(1)}, f32[4096]{0:T(1024)}, u32[]{:S(2)}) copy-start(f32[4096]{0:T(1024)} %param.23) | copy-start | bytes 49156
  218.6 165.3 %all-reduce.3.cloned.1.call-start = ((), (), s32[]{:S(2)}) async-start(), calls=%async_computation.8 | async-start | bytes 2097152 | tf_op jit(solution)/shard_map/psum | solution.py:97
  299.6 6.8 %copy-start.9 = (f32[256]{0:T(256)S(1)}, f32[256]{0:T(256)}, u32[]{:S(2)}) copy-start(f32[256]{0:T(256)} %param.27) | copy-start | bytes 3076
  383.9 3.5 copy-start.1
  387.4 16.2 %copy-start.7 = (bf16[256,512]{1,0:T(8,128)(2,1)S(1)}, bf16[256,512]{1,0:T(8,128)(2,1)}, u32[]{:S(2)}) copy-start(bf16[256,512]{1,0:T(8,128)(2,1)} %get-tuple-element.28) | copy-start | bytes 786436
  392.8 4.3 collective-permute-start
  397.1 5.0 collective-permute-start.1
  402.2 11.7 %collective-permute-start.2 = (bf16[256,512]{1,0:T(8,128)(2,1)S(1)}, bf16[256,512]{1,0:T(8,128)(2,1)S(1)}, u32[]{:S(2)}, u32[]{:S(2)}) collective-permute-start(bf16[256,512]{1,0:T(8,128)(2,1)S(1)} %maximum_select_fusion.8), channel_id=1, source_target_pairs={{0,4},{1,5},{2,6},{3,7},{4,0},{5,1},{6,2},{7,3},{8,12},{9,13},{10,... | collective-permute-start | bytes 786440 | tf_op jit(solution)/shard_map/ppermute | solution.py:18
  414.4 32.5 %slice-start.2 = ((s8[8388608]{0:T(1024)(128)(4,1)}), s8[4194304]{0:T(1024)(128)(4,1)S(1)}, s32[]{:S(2)}) async-start(s8[8388608]{0:T(1024)(128)(4,1)} %bitcast.83), calls=%async_computation.11 | async-start | bytes 8388608
  414.4 20.9 %copy-start.6 = (bf16[256,512]{1,0:T(8,128)(2,1)S(1)}, bf16[256,512]{1,0:T(8,128)(2,1)}, u32[]{:S(2)}) copy-start(bf16[256,512]{1,0:T(8,128)(2,1)} %get-tuple-element.27) | copy-start | bytes 786436
  414.4 32.5 %slice-start.3 = ((s8[8388608]{0:T(1024)(128)(4,1)}), s8[4194304]{0:T(1024)(128)(4,1)S(1)}, s32[]{:S(2)}) async-start(s8[8388608]{0:T(1024)(128)(4,1)} %bitcast.83), calls=%async_computation.12 | async-start | bytes 8388608
  425.5 4.3 collective-permute-start.3
  429.9 5.0 collective-permute-start.4
  435.0 11.4 %collective-permute-start.5 = (bf16[256,512]{1,0:T(8,128)(2,1)S(1)}, bf16[256,512]{1,0:T(8,128)(2,1)S(1)}, u32[]{:S(2)}, u32[]{:S(2)}) collective-permute-start(bf16[256,512]{1,0:T(8,128)(2,1)S(1)} %maximum_select_fusion.9), channel_id=1, source_target_pairs={{0,4},{1,5},{2,6},{3,7},{4,0},{5,1},{6,2},{7,3},{8,12},{9,13},{10,... | collective-permute-start | bytes 786440 | tf_op jit(solution)/shard_map/ppermute | solution.py:18
  446.9 26.6 %slice-start = ((s8[8388608]{0:T(1024)(128)(4,1)}), s8[4194304]{0:T(1024)(128)(4,1)S(1)}, s32[]{:S(2)}) async-start(s8[8388608]{0:T(1024)(128)(4,1)} %bitcast.81), calls=%async_computation.9 | async-start | bytes 8388608
  446.9 15.0 %copy-start.5 = (bf16[256,512]{1,0:T(8,128)(2,1)S(1)}, bf16[256,512]{1,0:T(8,128)(2,1)}, u32[]{:S(2)}) copy-start(bf16[256,512]{1,0:T(8,128)(2,1)} %get-tuple-element.26) | copy-start | bytes 786436
  446.9 26.6 %slice-start.1 = ((s8[8388608]{0:T(1024)(128)(4,1)}), s8[4194304]{0:T(1024)(128)(4,1)S(1)}, s32[]{:S(2)}) async-start(s8[8388608]{0:T(1024)(128)(4,1)} %bitcast.81), calls=%async_computation.10 | async-start | bytes 8388608
  452.3 4.3 collective-permute-start.6
  456.7 5.0 collective-permute-start.7
  461.8 11.3 %collective-permute-start.8 = (bf16[256,512]{1,0:T(8,128)(2,1)S(1)}, bf16[256,512]{1,0:T(8,128)(2,1)S(1)}, u32[]{:S(2)}, u32[]{:S(2)}) collective-permute-start(bf16[256,512]{1,0:T(8,128)(2,1)S(1)} %maximum_select_fusion.10), channel_id=1, source_target_pairs={{0,4},{1,5},{2,6},{3,7},{4,0},{5,1},{6,2},{7,3},{8,12},{9,13},{10,... | collective-permute-start | bytes 786440 | tf_op jit(solution)/shard_map/ppermute | solution.py:18
  473.5 25.9 %copy-start.4 = (f32[64,512]{1,0:T(8,128)S(1)}, f32[64,512]{1,0:T(8,128)}, u32[]{:S(2)}) copy-start(f32[64,512]{1,0:T(8,128)} %param.15) | copy-start | bytes 393220
  473.5 27.6 %copy-start.12 = (s32[64]{0:T(128)S(1)}, s32[64]{0:T(128)}, u32[]{:S(2)}) copy-start(s32[64]{0:T(128)} %param.22) | copy-start | bytes 772
  479.1 4.3 collective-permute-start.9
  483.5 5.0 collective-permute-start.10
  488.6 10.9 %collective-permute-start.11 = (bf16[256,512]{1,0:T(8,128)(2,1)S(1)}, bf16[256,512]{1,0:T(8,128)(2,1)S(1)}, u32[]{:S(2)}, u32[]{:S(2)}) collective-permute-start(bf16[256,512]{1,0:T(8,128)(2,1)S(1)} %maximum_select_fusion.11), channel_id=1, source_target_pairs={{0,4},{1,5},{2,6},{3,7},{4,0},{5,1},{6,2},{7,3},{8,12},{9,13},{10,... | collective-permute-start | bytes 786440 | tf_op jit(solution)/shard_map/ppermute | solution.py:18
Sparse Core Ops, SparseCore 0:
  13.6 66.9 reduce-scatter.12
  85.1 63.0 reduce-scatter.14
  151.9 63.1 reduce-scatter.16
  218.7 63.0 reduce-scatter.18
  306.5 77.3 all-reduce.2
